TPU v7x, 32 devices: a whole 2x2x4 slice. The times are simulated.
32 devices in a mesh: gx: 4 (over x, core), gy: 2 (over y), gz: 4 (over z).
Axes of the slice: x: 2, y: 2, z: 4, core: 2. Of those that a mesh axis runs over, the one named last changes fastest.
Arguments:
- solution: float32 [16, 8, 16, 256], P(None, 'gx', 'gz', 'gy'), may hold values from -0.6 to 0.6
- residual: float32 [16, 8, 16, 256], P(None, 'gx', 'gz', 'gy'), may hold values from -6 to 6
- direction_prev: float32 [16, 8, 16, 256], P(None, 'gx', 'gz', 'gy'), may hold values from -0.3 to 0.3, as said below
- image_prev: float32 [16, 8, 16, 256], P(None, 'gx', 'gz', 'gy'), may hold values from -9 to 9, as said below
- gram_prev: float32 [16, 16], replicated, may hold values from -32768 to 32768, as said below
Outputs:
- solution_new: float32 [16, 8, 16, 256], P(None, 'gx', 'gz', 'gy')
- residual_new: float32 [16, 8, 16, 256], P(None, 'gx', 'gz', 'gy')
- direction: float32 [16, 8, 16, 256], P(None, 'gx', 'gz', 'gy')
Inputs may be any that keep to these rules, and one draw needn't show every extreme that they name: direction_prev is a field of order 0.05. image_prev equals A direction_prev, computed in float32. gram_prev is symmetric and positive definite.
All inputs are finite; a program needn't handle non-finite values.
Results may differ from a plain program's by a relative error of at most 0.0001.
Values sent between devices are 32-bit elements; how exact they have to be, the bound alone decides.
No kernel may reach another device: no remote copies, remote signals or barrier semaphores. Data moves between devices by JAX's collectives and lax.ppermute only.
A program may use at most 64 MiB of HBM per device.

v0:
```python
import jax
import jax.numpy as jnp
from jax import lax
from jax.sharding import PartitionSpec as P


def with_halo(value, sides, width):
    for axis, dim in sides:
        devices, length = (lax.axis_size(axis), value.shape[dim])
        up = [(i, (i + 1) % devices) for i in range(devices - 1)]
        down = [(j, i) for i, j in up]
        last = lax.slice_in_dim(value, length - width, length, axis=dim)
        first = lax.slice_in_dim(value, 0, width, axis=dim)
        before = lax.ppermute(last, axis, up)
        after = lax.ppermute(first, axis, down)
        value = jnp.concatenate([before, value, after], axis=dim)
    return value


def box_sum(padded):
    total = padded[:, :-2] + padded[:, 1:-1] + padded[:, 2:]
    total = total[:, :, :-2] + total[:, :, 1:-1] + total[:, :, 2:]
    return total[:, :, :, :-2] + total[:, :, :, 1:-1] + total[:, :, :, 2:]


def colors_of(shape):
    first = lax.broadcasted_iota(jnp.int32, shape, 1) % 2
    second = lax.broadcasted_iota(jnp.int32, shape, 2) % 2
    third = lax.broadcasted_iota(jnp.int32, shape, 3) % 2
    return 4 * first + 2 * second + third


def local_gram(left, right):
    return jnp.einsum("kxzy,lxzy->kl", left, right, precision=lax.Precision.HIGHEST)


def combine(field, mixing):
    return jnp.einsum("kxzy,kl->lxzy", field, mixing, precision=lax.Precision.HIGHEST)


def small_dot(left, right):
    return jnp.dot(left, right, precision=lax.Precision.HIGHEST)


def spd_solve(matrix, target):
    order = matrix.shape[0]
    sym = 0.5 * (matrix + matrix.T)
    lower = jnp.zeros_like(sym)
    for col in range(order):
        column = sym[col:, col] - jnp.sum(lower[col:, :col] * lower[col, :col][None, :], axis=1)
        pivot = jnp.sqrt(column[0])
        lower = lower.at[col:, col].set(column / pivot)
    middle = jnp.zeros_like(target)
    for row in range(order):
        value = target[row] - jnp.sum(lower[row, :row][:, None] * middle[:row], axis=0)
        middle = middle.at[row].set(value / lower[row, row])
    answer = jnp.zeros_like(target)
    for row in range(order - 1, -1, -1):
        value = middle[row] - jnp.sum(lower[row + 1 :, row][:, None] * answer[row + 1 :], axis=0)
        answer = answer.at[row].set(value / lower[row, row])
    return answer


def sweep_box(field):
    padded = with_halo(field, (("gx", 1), ("gy", 3), ("gz", 2)), 1)
    return box_sum(padded)


def body(solution, residual, direction_prev, image_prev, gram_prev):
    colors = colors_of(residual.shape)
    smoothed = jnp.where(colors == 0, residual / 26.0, jnp.float32(0.0))
    for shade in list(range(1, 8)) + list(range(6, -1, -1)):
        boxed = sweep_box(smoothed)
        smoothed = jnp.where(colors == shade, (residual + boxed - smoothed) / 26.0, smoothed)
    padded = with_halo(smoothed, (("gx", 1), ("gy", 3), ("gz", 2)), 1)
    image = 27.0 * smoothed - box_sum(padded)
    sums = (
        local_gram(smoothed, residual),
        local_gram(smoothed, image),
        local_gram(smoothed, image_prev),
        local_gram(direction_prev, image),
        local_gram(direction_prev, image_prev),
    )
    gram_zr, gram_zw, gram_zq, gram_pw, gram_pq = lax.psum(
        (sums[0], sums[1], sums[2], sums[3], sums[4]), ("gx", "gy", "gz")
    )
    beta_mix = spd_solve(gram_prev, gram_zr)
    direction = smoothed + combine(direction_prev, beta_mix)
    image_new = image + combine(image_prev, beta_mix)
    curvature = gram_zw + small_dot(gram_zq, beta_mix) + small_dot(beta_mix.T, gram_pw)
    curvature = curvature + small_dot(small_dot(beta_mix.T, gram_pq), beta_mix)
    alpha_step = spd_solve(curvature, gram_zr)
    solution_new = solution + combine(direction, alpha_step)
    residual_new = residual - combine(image_new, alpha_step)
    return (solution_new, residual_new, direction)


def solution(mesh):
    in_specs = (
        P(None, "gx", "gz", "gy"),
        P(None, "gx", "gz", "gy"),
        P(None, "gx", "gz", "gy"),
        P(None, "gx", "gz", "gy"),
        P(),
    )
    out_specs = (P(None, "gx", "gz", "gy"), P(None, "gx", "gz", "gy"), P(None, "gx", "gz", "gy"))
    return jax.shard_map(body, mesh=mesh, in_specs=in_specs, out_specs=out_specs, check_vma=False)
```

profile of v0, /device:TPU:0, one launch (start us, length us, event | category | flops | bytes accessed | tf_op | source)
XLA Modules:
  0.0 495.2 jit_solution(12396959425501181571)
XLA Ops:
  21.4 4.9 collective-permute-start.2
  30.6 6.1 %collective-permute-start.4 = (f32[16,4,1,130]{3,0,2,1:T(8,128)S(1)}, f32[16,4,1,130]{3,0,2,1:T(8,128)S(1)}, u32[]{:S(2)}, u32[]{:S(2)}) collective-permute-start(f32[16,4,1,130]{3,0,2,1:T(8,128)S(1)} %get-tuple-element.1202), channel_id=1, source_target_pairs={{0,1},{1,2},{2,3},{4,5},{5,6},{6,7},{8,9},{9,10},{10,11},{12,13},{... | collective-permute-start | bytes 99848 | tf_op jit(solution)/shard_map/ppermute | solution.py:14
  46.4 4.6 collective-permute-start.8
  55.6 4.8 collective-permute-start.10
  69.3 4.6 collective-permute-start.14
  78.5 4.9 collective-permute-start.16
  92.6 4.6 collective-permute-start.20
  101.1 5.0 %collective-permute-start.22 = (f32[16,4,1,130]{3,0,2,1:T(8,128)S(1)}, f32[16,4,1,130]{3,0,2,1:T(8,128)S(1)}, u32[]{:S(2)}, u32[]{:S(2)}) collective-permute-start(f32[16,4,1,130]{3,0,2,1:T(8,128)S(1)} %get-tuple-element.1196), channel_id=1, source_target_pairs={{0,1},{1,2},{2,3},{4,5},{5,6},{6,7},{8,9},{9,10},{10,11},{12,13},{... | collective-permute-start | bytes 99848 | tf_op jit(solution)/shard_map/ppermute | solution.py:14
  115.2 4.6 collective-permute-start.26
  123.7 5.0 %collective-permute-start.28 = (f32[16,4,1,130]{3,0,2,1:T(8,128)S(1)}, f32[16,4,1,130]{3,0,2,1:T(8,128)S(1)}, u32[]{:S(2)}, u32[]{:S(2)}) collective-permute-start(f32[16,4,1,130]{3,0,2,1:T(8,128)S(1)} %get-tuple-element.1194), channel_id=1, source_target_pairs={{0,1},{1,2},{2,3},{4,5},{5,6},{6,7},{8,9},{9,10},{10,11},{12,13},{... | collective-permute-start | bytes 99848 | tf_op jit(solution)/shard_map/ppermute | solution.py:14
  132.2 4.9 collective-permute-start.30
  139.4 4.6 collective-permute-start.32
  147.9 4.6 collective-permute-start.34
  156.0 5.3 %collective-permute-start.36 = (f32[16,1,4,128]{3,0,2,1:T(8,128)S(1)}, f32[16,1,4,128]{3,0,2,1:T(8,128)S(1)}, u32[]{:S(2)}, u32[]{:S(2)}) collective-permute-start(f32[16,1,4,128]{3,0,2,1:T(8,128)S(1)} %get-tuple-element.1250), channel_id=1, source_target_pairs={{0,8},{8,16},{16,24},{1,9},{9,17},{17,25},{2,10},{10,18},{18,26},{... | collective-permute-start | bytes 98312 | tf_op jit(solution)/shard_map/ppermute | solution.py:14
  172.1 4.6 collective-permute-start.40
  180.3 5.3 %collective-permute-start.42 = (f32[16,1,4,128]{3,0,2,1:T(8,128)S(1)}, f32[16,1,4,128]{3,0,2,1:T(8,128)S(1)}, u32[]{:S(2)}, u32[]{:S(2)}) collective-permute-start(f32[16,1,4,128]{3,0,2,1:T(8,128)S(1)} %get-tuple-element.1248), channel_id=1, source_target_pairs={{0,8},{8,16},{16,24},{1,9},{9,17},{17,25},{2,10},{10,18},{18,26},{... | collective-permute-start | bytes 98312 | tf_op jit(solution)/shard_map/ppermute | solution.py:14
  196.3 4.8 collective-permute-start.46
  204.5 5.3 %collective-permute-start.48 = (f32[16,1,4,128]{3,0,2,1:T(8,128)S(1)}, f32[16,1,4,128]{3,0,2,1:T(8,128)S(1)}, u32[]{:S(2)}, u32[]{:S(2)}) collective-permute-start(f32[16,1,4,128]{3,0,2,1:T(8,128)S(1)} %get-tuple-element.1246), channel_id=1, source_target_pairs={{0,8},{8,16},{16,24},{1,9},{9,17},{17,25},{2,10},{10,18},{18,26},{... | collective-permute-start | bytes 98312 | tf_op jit(solution)/shard_map/ppermute | solution.py:14
  220.5 4.6 collective-permute-start.52
  228.7 5.3 %collective-permute-start.54 = (f32[16,1,4,128]{3,0,2,1:T(8,128)S(1)}, f32[16,1,4,128]{3,0,2,1:T(8,128)S(1)}, u32[]{:S(2)}, u32[]{:S(2)}) collective-permute-start(f32[16,1,4,128]{3,0,2,1:T(8,128)S(1)} %get-tuple-element.1244), channel_id=1, source_target_pairs={{0,8},{8,16},{16,24},{1,9},{9,17},{17,25},{2,10},{10,18},{18,26},{... | collective-permute-start | bytes 98312 | tf_op jit(solution)/shard_map/ppermute | solution.py:14
  244.8 4.6 collective-permute-start.58
  253.0 5.3 %collective-permute-start.60 = (f32[16,1,4,128]{3,0,2,1:T(8,128)S(1)}, f32[16,1,4,128]{3,0,2,1:T(8,128)S(1)}, u32[]{:S(2)}, u32[]{:S(2)}) collective-permute-start(f32[16,1,4,128]{3,0,2,1:T(8,128)S(1)} %get-tuple-element.1242), channel_id=1, source_target_pairs={{0,8},{8,16},{16,24},{1,9},{9,17},{17,25},{2,10},{10,18},{18,26},{... | collective-permute-start | bytes 98312 | tf_op jit(solution)/shard_map/ppermute | solution.py:14
  269.0 4.6 collective-permute-start.64
  277.2 5.3 %collective-permute-start.66 = (f32[16,1,4,128]{3,0,2,1:T(8,128)S(1)}, f32[16,1,4,128]{3,0,2,1:T(8,128)S(1)}, u32[]{:S(2)}, u32[]{:S(2)}) collective-permute-start(f32[16,1,4,128]{3,0,2,1:T(8,128)S(1)} %get-tuple-element.1240), channel_id=1, source_target_pairs={{0,8},{8,16},{16,24},{1,9},{9,17},{17,25},{2,10},{10,18},{18,26},{... | collective-permute-start | bytes 98312 | tf_op jit(solution)/shard_map/ppermute | solution.py:14
  293.2 4.6 collective-permute-start.70
  301.4 5.3 %collective-permute-start.72 = (f32[16,1,4,128]{3,0,2,1:T(8,128)S(1)}, f32[16,1,4,128]{3,0,2,1:T(8,128)S(1)}, u32[]{:S(2)}, u32[]{:S(2)}) collective-permute-start(f32[16,1,4,128]{3,0,2,1:T(8,128)S(1)} %get-tuple-element.1238), channel_id=1, source_target_pairs={{0,8},{8,16},{16,24},{1,9},{9,17},{17,25},{2,10},{10,18},{18,26},{... | collective-permute-start | bytes 98312 | tf_op jit(solution)/shard_map/ppermute | solution.py:14
  317.5 4.6 collective-permute-start.76
  325.6 5.3 %collective-permute-start.78 = (f32[16,1,4,128]{3,0,2,1:T(8,128)S(1)}, f32[16,1,4,128]{3,0,2,1:T(8,128)S(1)}, u32[]{:S(2)}, u32[]{:S(2)}) collective-permute-start(f32[16,1,4,128]{3,0,2,1:T(8,128)S(1)} %get-tuple-element.1236), channel_id=1, source_target_pairs={{0,8},{8,16},{16,24},{1,9},{9,17},{17,25},{2,10},{10,18},{18,26},{... | collective-permute-start | bytes 98312 | tf_op jit(solution)/shard_map/ppermute | solution.py:14
  341.7 4.6 collective-permute-start.82
  349.9 5.3 %collective-permute-start.84 = (f32[16,1,4,128]{3,0,2,1:T(8,128)S(1)}, f32[16,1,4,128]{3,0,2,1:T(8,128)S(1)}, u32[]{:S(2)}, u32[]{:S(2)}) collective-permute-start(f32[16,1,4,128]{3,0,2,1:T(8,128)S(1)} %get-tuple-element.1234), channel_id=1, source_target_pairs={{0,8},{8,16},{16,24},{1,9},{9,17},{17,25},{2,10},{10,18},{18,26},{... | collective-permute-start | bytes 98312 | tf_op jit(solution)/shard_map/ppermute | solution.py:14
  367.0 4.6 collective-permute-start.88
  374.2 47.6 %all-reduce.6 = (f32[16,16]{1,0:T(8,128)S(1)}, f32[16,16]{1,0:T(8,128)S(1)}, f32[16,16]{1,0:T(8,128)S(1)}, f32[16,16]{0,1:T(8,128)S(1)}, f32[16,16]{1,0:T(8,128)S(1)}) all-reduce(f32[16,16]{1,0:T(8,128)S(1)} %convolution_bitcast_fusion.4, ...), channel_id=1, replica_groups=mesh['gx'=4,'gy'=2,'gz'=4] {'gx','gy','gz'}, use_global_device_ids=true, to_apply=%region_0.1 | all-reduce | flops 1280 | bytes 10240 | tf_op jit(solution)/shard_map/psum | solution.py:84
  (741 shorter events, 284.0 us)
Async XLA Ops:
  1.7 18.3 %collective-permute-start.1 = (f32[16,1,4,128]{3,0,2,1:T(8,128)S(1)}, f32[16,1,4,128]{3,0,2,1:T(8,128)S(1)}, u32[]{:S(2)}, u32[]{:S(2)}) collective-permute-start(f32[16,1,4,128]{3,0,2,1:T(8,128)S(1)} %get-tuple-element.1263), channel_id=1, source_target_pairs={{8,0},{16,8},{24,16},{9,1},{17,9},{25,17},{10,2},{18,10},{26,18},{... | collective-permute-start | bytes 98312 | tf_op jit(solution)/shard_map/ppermute | solution.py:15
  3.0 17.0 %collective-permute-start = (f32[16,1,4,128]{3,0,2,1:T(8,128)S(1)}, f32[16,1,4,128]{3,0,2,1:T(8,128)S(1)}, u32[]{:S(2)}, u32[]{:S(2)}) collective-permute-start(f32[16,1,4,128]{3,0,2,1:T(8,128)S(1)} %get-tuple-element.1262), channel_id=1, source_target_pairs={{0,8},{8,16},{16,24},{1,9},{9,17},{17,25},{2,10},{10,18},{18,26},{... | collective-permute-start | bytes 98312 | tf_op jit(solution)/shard_map/ppermute | solution.py:14
  20.1 7.4 %collective-permute-start.3 = (f32[16,4,4,1]{3,0,2,1:T(8,128)S(1)}, f32[16,4,4,1]{3,0,2,1:T(8,128)S(1)}, u32[]{:S(2)}, u32[]{:S(2)}) collective-permute-start(f32[16,4,4,1]{3,0,2,1:T(8,128)S(1)} %get-tuple-element.1233), channel_id=1, source_target_pairs={{4,0},{5,1},{6,2},{7,3},{12,8},{13,9},{14,10},{15,11},{20,16},{21,... | collective-permute-start | bytes 3080 | tf_op jit(solution)/shard_map/ppermute | solution.py:15
  21.4 7.8 %collective-permute-start.2 = (f32[16,4,4,1]{3,0,2,1:T(8,128)S(1)}, f32[16,4,4,1]{3,0,2,1:T(8,128)S(1)}, u32[]{:S(2)}, u32[]{:S(2)}) collective-permute-start(f32[16,4,4,1]{3,0,2,1:T(8,128)S(1)} %get-tuple-element.1232), channel_id=1, source_target_pairs={{0,4},{1,5},{2,6},{3,7},{8,12},{9,13},{10,14},{11,15},{16,20},{17,... | collective-permute-start | bytes 3080 | tf_op jit(solution)/shard_map/ppermute | solution.py:14
  29.3 7.8 %collective-permute-start.5 = (f32[16,4,1,130]{3,0,2,1:T(8,128)S(1)}, f32[16,4,1,130]{3,0,2,1:T(8,128)S(1)}, u32[]{:S(2)}, u32[]{:S(2)}) collective-permute-start(f32[16,4,1,130]{3,0,2,1:T(8,128)S(1)} %get-tuple-element.1203), channel_id=1, source_target_pairs={{1,0},{2,1},{3,2},{5,4},{6,5},{7,6},{9,8},{10,9},{11,10},{13,12},{... | collective-permute-start | bytes 99848 | tf_op jit(solution)/shard_map/ppermute | solution.py:15
  30.6 8.0 %collective-permute-start.4 = (f32[16,4,1,130]{3,0,2,1:T(8,128)S(1)}, f32[16,4,1,130]{3,0,2,1:T(8,128)S(1)}, u32[]{:S(2)}, u32[]{:S(2)}) collective-permute-start(f32[16,4,1,130]{3,0,2,1:T(8,128)S(1)} %get-tuple-element.1202), channel_id=1, source_target_pairs={{0,1},{1,2},{2,3},{4,5},{5,6},{6,7},{8,9},{9,10},{10,11},{12,13},{... | collective-permute-start | bytes 99848 | tf_op jit(solution)/shard_map/ppermute | solution.py:14
  45.1 7.9 %collective-permute-start.9 = (f32[16,4,4,1]{3,0,2,1:T(8,128)S(1)}, f32[16,4,4,1]{3,0,2,1:T(8,128)S(1)}, u32[]{:S(2)}, u32[]{:S(2)}) collective-permute-start(f32[16,4,4,1]{3,0,2,1:T(8,128)S(1)} %get-tuple-element.1231), channel_id=1, source_target_pairs={{4,0},{5,1},{6,2},{7,3},{12,8},{13,9},{14,10},{15,11},{20,16},{21,... | collective-permute-start | bytes 3080 | tf_op jit(solution)/shard_map/ppermute | solution.py:15
  46.4 7.8 %collective-permute-start.8 = (f32[16,4,4,1]{3,0,2,1:T(8,128)S(1)}, f32[16,4,4,1]{3,0,2,1:T(8,128)S(1)}, u32[]{:S(2)}, u32[]{:S(2)}) collective-permute-start(f32[16,4,4,1]{3,0,2,1:T(8,128)S(1)} %get-tuple-element.1230), channel_id=1, source_target_pairs={{0,4},{1,5},{2,6},{3,7},{8,12},{9,13},{10,14},{11,15},{16,20},{17,... | collective-permute-start | bytes 3080 | tf_op jit(solution)/shard_map/ppermute | solution.py:14
  68.0 7.4 %collective-permute-start.15 = (f32[16,4,4,1]{3,0,2,1:T(8,128)S(1)}, f32[16,4,4,1]{3,0,2,1:T(8,128)S(1)}, u32[]{:S(2)}, u32[]{:S(2)}) collective-permute-start(f32[16,4,4,1]{3,0,2,1:T(8,128)S(1)} %get-tuple-element.1229), channel_id=1, source_target_pairs={{4,0},{5,1},{6,2},{7,3},{12,8},{13,9},{14,10},{15,11},{20,16},{21,... | collective-permute-start | bytes 3080 | tf_op jit(solution)/shard_map/ppermute | solution.py:15
  69.3 7.8 %collective-permute-start.14 = (f32[16,4,4,1]{3,0,2,1:T(8,128)S(1)}, f32[16,4,4,1]{3,0,2,1:T(8,128)S(1)}, u32[]{:S(2)}, u32[]{:S(2)}) collective-permute-start(f32[16,4,4,1]{3,0,2,1:T(8,128)S(1)} %get-tuple-element.1228), channel_id=1, source_target_pairs={{0,4},{1,5},{2,6},{3,7},{8,12},{9,13},{10,14},{11,15},{16,20},{17,... | collective-permute-start | bytes 3080 | tf_op jit(solution)/shard_map/ppermute | solution.py:14
  77.2 7.2 %collective-permute-start.17 = (f32[16,4,1,130]{3,0,2,1:T(8,128)S(1)}, f32[16,4,1,130]{3,0,2,1:T(8,128)S(1)}, u32[]{:S(2)}, u32[]{:S(2)}) collective-permute-start(f32[16,4,1,130]{3,0,2,1:T(8,128)S(1)} %get-tuple-element.1199), channel_id=1, source_target_pairs={{1,0},{2,1},{3,2},{5,4},{6,5},{7,6},{9,8},{10,9},{11,10},{13,12},{... | collective-permute-start | bytes 99848 | tf_op jit(solution)/shard_map/ppermute | solution.py:15
  78.5 7.1 %collective-permute-start.16 = (f32[16,4,1,130]{3,0,2,1:T(8,128)S(1)}, f32[16,4,1,130]{3,0,2,1:T(8,128)S(1)}, u32[]{:S(2)}, u32[]{:S(2)}) collective-permute-start(f32[16,4,1,130]{3,0,2,1:T(8,128)S(1)} %get-tuple-element.1198), channel_id=1, source_target_pairs={{0,1},{1,2},{2,3},{4,5},{5,6},{6,7},{8,9},{9,10},{10,11},{12,13},{... | collective-permute-start | bytes 99848 | tf_op jit(solution)/shard_map/ppermute | solution.py:14
  91.3 6.9 %collective-permute-start.21 = (f32[16,4,4,1]{3,0,2,1:T(8,128)S(1)}, f32[16,4,4,1]{3,0,2,1:T(8,128)S(1)}, u32[]{:S(2)}, u32[]{:S(2)}) collective-permute-start(f32[16,4,4,1]{3,0,2,1:T(8,128)S(1)} %get-tuple-element.1227), channel_id=1, source_target_pairs={{4,0},{5,1},{6,2},{7,3},{12,8},{13,9},{14,10},{15,11},{20,16},{21,... | collective-permute-start | bytes 3080 | tf_op jit(solution)/shard_map/ppermute | solution.py:15
  92.6 7.1 %collective-permute-start.20 = (f32[16,4,4,1]{3,0,2,1:T(8,128)S(1)}, f32[16,4,4,1]{3,0,2,1:T(8,128)S(1)}, u32[]{:S(2)}, u32[]{:S(2)}) collective-permute-start(f32[16,4,4,1]{3,0,2,1:T(8,128)S(1)} %get-tuple-element.1226), channel_id=1, source_target_pairs={{0,4},{1,5},{2,6},{3,7},{8,12},{9,13},{10,14},{11,15},{16,20},{17,... | collective-permute-start | bytes 3080 | tf_op jit(solution)/shard_map/ppermute | solution.py:14
  101.1 7.0 %collective-permute-start.22 = (f32[16,4,1,130]{3,0,2,1:T(8,128)S(1)}, f32[16,4,1,130]{3,0,2,1:T(8,128)S(1)}, u32[]{:S(2)}, u32[]{:S(2)}) collective-permute-start(f32[16,4,1,130]{3,0,2,1:T(8,128)S(1)} %get-tuple-element.1196), channel_id=1, source_target_pairs={{0,1},{1,2},{2,3},{4,5},{5,6},{6,7},{8,9},{9,10},{10,11},{12,13},{... | collective-permute-start | bytes 99848 | tf_op jit(solution)/shard_map/ppermute | solution.py:14
  113.9 6.9 %collective-permute-start.27 = (f32[16,4,4,1]{3,0,2,1:T(8,128)S(1)}, f32[16,4,4,1]{3,0,2,1:T(8,128)S(1)}, u32[]{:S(2)}, u32[]{:S(2)}) collective-permute-start(f32[16,4,4,1]{3,0,2,1:T(8,128)S(1)} %get-tuple-element.1225), channel_id=1, source_target_pairs={{4,0},{5,1},{6,2},{7,3},{12,8},{13,9},{14,10},{15,11},{20,16},{21,... | collective-permute-start | bytes 3080 | tf_op jit(solution)/shard_map/ppermute | solution.py:15
  115.2 7.1 %collective-permute-start.26 = (f32[16,4,4,1]{3,0,2,1:T(8,128)S(1)}, f32[16,4,4,1]{3,0,2,1:T(8,128)S(1)}, u32[]{:S(2)}, u32[]{:S(2)}) collective-permute-start(f32[16,4,4,1]{3,0,2,1:T(8,128)S(1)} %get-tuple-element.1224), channel_id=1, source_target_pairs={{0,4},{1,5},{2,6},{3,7},{8,12},{9,13},{10,14},{11,15},{16,20},{17,... | collective-permute-start | bytes 3080 | tf_op jit(solution)/shard_map/ppermute | solution.py:14
  123.7 6.9 %collective-permute-start.28 = (f32[16,4,1,130]{3,0,2,1:T(8,128)S(1)}, f32[16,4,1,130]{3,0,2,1:T(8,128)S(1)}, u32[]{:S(2)}, u32[]{:S(2)}) collective-permute-start(f32[16,4,1,130]{3,0,2,1:T(8,128)S(1)} %get-tuple-element.1194), channel_id=1, source_target_pairs={{0,1},{1,2},{2,3},{4,5},{5,6},{6,7},{8,9},{9,10},{10,11},{12,13},{... | collective-permute-start | bytes 99848 | tf_op jit(solution)/shard_map/ppermute | solution.py:14
  138.1 6.9 %collective-permute-start.33 = (f32[16,4,4,1]{3,0,2,1:T(8,128)S(1)}, f32[16,4,4,1]{3,0,2,1:T(8,128)S(1)}, u32[]{:S(2)}, u32[]{:S(2)}) collective-permute-start(f32[16,4,4,1]{3,0,2,1:T(8,128)S(1)} %get-tuple-element.1223), channel_id=1, source_target_pairs={{4,0},{5,1},{6,2},{7,3},{12,8},{13,9},{14,10},{15,11},{20,16},{21,... | collective-permute-start | bytes 3080 | tf_op jit(solution)/shard_map/ppermute | solution.py:15
  139.4 7.1 %collective-permute-start.32 = (f32[16,4,4,1]{3,0,2,1:T(8,128)S(1)}, f32[16,4,4,1]{3,0,2,1:T(8,128)S(1)}, u32[]{:S(2)}, u32[]{:S(2)}) collective-permute-start(f32[16,4,4,1]{3,0,2,1:T(8,128)S(1)} %get-tuple-element.1222), channel_id=1, source_target_pairs={{0,4},{1,5},{2,6},{3,7},{8,12},{9,13},{10,14},{11,15},{16,20},{17,... | collective-permute-start | bytes 3080 | tf_op jit(solution)/shard_map/ppermute | solution.py:14
  163.6 7.1 %collective-permute-start.38 = (f32[16,4,4,1]{3,0,2,1:T(8,128)S(1)}, f32[16,4,4,1]{3,0,2,1:T(8,128)S(1)}, u32[]{:S(2)}, u32[]{:S(2)}) collective-permute-start(f32[16,4,4,1]{3,0,2,1:T(8,128)S(1)} %get-tuple-element.1220), channel_id=1, source_target_pairs={{0,4},{1,5},{2,6},{3,7},{8,12},{9,13},{10,14},{11,15},{16,20},{17,... | collective-permute-start | bytes 3080 | tf_op jit(solution)/shard_map/ppermute | solution.py:14
  187.8 7.1 %collective-permute-start.44 = (f32[16,4,4,1]{3,0,2,1:T(8,128)S(1)}, f32[16,4,4,1]{3,0,2,1:T(8,128)S(1)}, u32[]{:S(2)}, u32[]{:S(2)}) collective-permute-start(f32[16,4,4,1]{3,0,2,1:T(8,128)S(1)} %get-tuple-element.1218), channel_id=1, source_target_pairs={{0,4},{1,5},{2,6},{3,7},{8,12},{9,13},{10,14},{11,15},{16,20},{17,... | collective-permute-start | bytes 3080 | tf_op jit(solution)/shard_map/ppermute | solution.py:14
  212.1 7.1 %collective-permute-start.50 = (f32[16,4,4,1]{3,0,2,1:T(8,128)S(1)}, f32[16,4,4,1]{3,0,2,1:T(8,128)S(1)}, u32[]{:S(2)}, u32[]{:S(2)}) collective-permute-start(f32[16,4,4,1]{3,0,2,1:T(8,128)S(1)} %get-tuple-element.1216), channel_id=1, source_target_pairs={{0,4},{1,5},{2,6},{3,7},{8,12},{9,13},{10,14},{11,15},{16,20},{17,... | collective-permute-start | bytes 3080 | tf_op jit(solution)/shard_map/ppermute | solution.py:14
  227.4 7.3 %collective-permute-start.55 = (f32[16,1,4,128]{3,0,2,1:T(8,128)S(1)}, f32[16,1,4,128]{3,0,2,1:T(8,128)S(1)}, u32[]{:S(2)}, u32[]{:S(2)}) collective-permute-start(f32[16,1,4,128]{3,0,2,1:T(8,128)S(1)} %get-tuple-element.1245), channel_id=1, source_target_pairs={{8,0},{16,8},{24,16},{9,1},{17,9},{25,17},{10,2},{18,10},{26,18},{... | collective-permute-start | bytes 98312 | tf_op jit(solution)/shard_map/ppermute | solution.py:15
  236.3 7.1 %collective-permute-start.56 = (f32[16,4,4,1]{3,0,2,1:T(8,128)S(1)}, f32[16,4,4,1]{3,0,2,1:T(8,128)S(1)}, u32[]{:S(2)}, u32[]{:S(2)}) collective-permute-start(f32[16,4,4,1]{3,0,2,1:T(8,128)S(1)} %get-tuple-element.1214), channel_id=1, source_target_pairs={{0,4},{1,5},{2,6},{3,7},{8,12},{9,13},{10,14},{11,15},{16,20},{17,... | collective-permute-start | bytes 3080 | tf_op jit(solution)/shard_map/ppermute | solution.py:14
  260.5 7.1 %collective-permute-start.62 = (f32[16,4,4,1]{3,0,2,1:T(8,128)S(1)}, f32[16,4,4,1]{3,0,2,1:T(8,128)S(1)}, u32[]{:S(2)}, u32[]{:S(2)}) collective-permute-start(f32[16,4,4,1]{3,0,2,1:T(8,128)S(1)} %get-tuple-element.1212), channel_id=1, source_target_pairs={{0,4},{1,5},{2,6},{3,7},{8,12},{9,13},{10,14},{11,15},{16,20},{17,... | collective-permute-start | bytes 3080 | tf_op jit(solution)/shard_map/ppermute | solution.py:14
  284.8 7.1 %collective-permute-start.68 = (f32[16,4,4,1]{3,0,2,1:T(8,128)S(1)}, f32[16,4,4,1]{3,0,2,1:T(8,128)S(1)}, u32[]{:S(2)}, u32[]{:S(2)}) collective-permute-start(f32[16,4,4,1]{3,0,2,1:T(8,128)S(1)} %get-tuple-element.1210), channel_id=1, source_target_pairs={{0,4},{1,5},{2,6},{3,7},{8,12},{9,13},{10,14},{11,15},{16,20},{17,... | collective-permute-start | bytes 3080 | tf_op jit(solution)/shard_map/ppermute | solution.py:14
  309.0 7.1 %collective-permute-start.74 = (f32[16,4,4,1]{3,0,2,1:T(8,128)S(1)}, f32[16,4,4,1]{3,0,2,1:T(8,128)S(1)}, u32[]{:S(2)}, u32[]{:S(2)}) collective-permute-start(f32[16,4,4,1]{3,0,2,1:T(8,128)S(1)} %get-tuple-element.1208), channel_id=1, source_target_pairs={{0,4},{1,5},{2,6},{3,7},{8,12},{9,13},{10,14},{11,15},{16,20},{17,... | collective-permute-start | bytes 3080 | tf_op jit(solution)/shard_map/ppermute | solution.py:14
  333.2 7.1 %collective-permute-start.80 = (f32[16,4,4,1]{3,0,2,1:T(8,128)S(1)}, f32[16,4,4,1]{3,0,2,1:T(8,128)S(1)}, u32[]{:S(2)}, u32[]{:S(2)}) collective-permute-start(f32[16,4,4,1]{3,0,2,1:T(8,128)S(1)} %get-tuple-element.1206), channel_id=1, source_target_pairs={{0,4},{1,5},{2,6},{3,7},{8,12},{9,13},{10,14},{11,15},{16,20},{17,... | collective-permute-start | bytes 3080 | tf_op jit(solution)/shard_map/ppermute | solution.py:14
  348.6 8.4 %collective-permute-start.85 = (f32[16,1,4,128]{3,0,2,1:T(8,128)S(1)}, f32[16,1,4,128]{3,0,2,1:T(8,128)S(1)}, u32[]{:S(2)}, u32[]{:S(2)}) collective-permute-start(f32[16,1,4,128]{3,0,2,1:T(8,128)S(1)} %get-tuple-element.1235), channel_id=1, source_target_pairs={{8,0},{16,8},{24,16},{9,1},{17,9},{25,17},{10,2},{18,10},{26,18},{... | collective-permute-start | bytes 98312 | tf_op jit(solution)/shard_map/ppermute | solution.py:15
  349.9 7.2 %collective-permute-start.84 = (f32[16,1,4,128]{3,0,2,1:T(8,128)S(1)}, f32[16,1,4,128]{3,0,2,1:T(8,128)S(1)}, u32[]{:S(2)}, u32[]{:S(2)}) collective-permute-start(f32[16,1,4,128]{3,0,2,1:T(8,128)S(1)} %get-tuple-element.1234), channel_id=1, source_target_pairs={{0,8},{8,16},{16,24},{1,9},{9,17},{17,25},{2,10},{10,18},{18,26},{... | collective-permute-start | bytes 98312 | tf_op jit(solution)/shard_map/ppermute | solution.py:14
  358.5 7.1 %collective-permute-start.86 = (f32[16,4,4,1]{3,0,2,1:T(8,128)S(1)}, f32[16,4,4,1]{3,0,2,1:T(8,128)S(1)}, u32[]{:S(2)}, u32[]{:S(2)}) collective-permute-start(f32[16,4,4,1]{3,0,2,1:T(8,128)S(1)} %get-tuple-element.1204), channel_id=1, source_target_pairs={{0,4},{1,5},{2,6},{3,7},{8,12},{9,13},{10,14},{11,15},{16,20},{17,... | collective-permute-start | bytes 3080 | tf_op jit(solution)/shard_map/ppermute | solution.py:14
  (63 other events, 596.6 us)
where the time goes:
time: 498 us; the launch traced here: 495 us
  starting transfers between devices  267 us (54%)
  waiting for transfers between devices  71.8 us (14%)
  other arithmetic  62.7 us (13%)
  blocking collectives  47.6 us (10%)
  local copies, waits for them, and re-layouts  32.4 us (7%)
  between operations  11.3 us (2%)
    ppermute x45, starting transfers between devices, with_halo(): before = lax.ppermute(last, axis, up)  209 us
    ppermute x45, starting transfers between devices, with_halo(): after = lax.ppermute(first, axis, down)  58.1 us
    ppermute x45, waiting for transfers between devices, with_halo(): before = lax.ppermute(last, axis, up)  54.6 us
    psum x1, blocking collectives, body(): lax.psum((sums[0], sums[1], sums[2], sums[3], sums[4]), ('gx', 'gy', 'gz'))  47.6 us
    div x30, other arithmetic, spd_solve(): answer = answer.at[row].set(value / lower[row, row])  20.1 us
    div x28, other arithmetic, spd_solve(): middle = middle.at[row].set(value / lower[row, row])  20.1 us
    ppermute x45, waiting for transfers between devices, with_halo(): after = lax.ppermute(first, axis, down)  17.2 us
  transfers between devices with their start and end apart: 90, of which 71 were waited for; matrix products, arithmetic and copies ran while one was open for 4% of the time, Pallas kernels for 0%

commit v1 on v0

--- a/solution.py
+++ b/solution.py
@@ -82,7 +82,7 @@
         local_gram(direction_prev, image_prev),
     )
     gram_zr, gram_zw, gram_zq, gram_pw, gram_pq = lax.psum(
-        (sums[0], sums[1], sums[2], sums[3], sums[4]), ("gx", "gy", "gz")
+        lax.psum((sums[0], sums[1], sums[2], sums[3], sums[4]), ("gy", "gz")), "gx"
     )
     beta_mix = spd_solve(gram_prev, gram_zr)
     direction = smoothed + combine(direction_prev, beta_mix)

time: 498 us -> 506 us (1.016)
  blocking collectives: 47.6 us -> 55 us
    psum x1 -> x2, blocking collectives: 47.6 us -> 55 us  [the longest x1 40.9 us: body(): lax.psum((sums[0], sums[1], sums[2], sums[3], sums[4]), ('gy', 'gz'))]
where the time goes in v1:
time: 506 us; the launch traced here: 503 us
  starting transfers between devices  267 us (53%)
  waiting for transfers between devices  71.8 us (14%)
  other arithmetic  62.7 us (12%)
  blocking collectives  55 us (11%)
  local copies, waits for them, and re-layouts  32.4 us (6%)
  between operations  11.3 us (2%)
    ppermute x45, starting transfers between devices, with_halo(): before = lax.ppermute(last, axis, up)  209 us
    ppermute x45, starting transfers between devices, with_halo(): after = lax.ppermute(first, axis, down)  58.1 us
    ppermute x45, waiting for transfers between devices, with_halo(): before = lax.ppermute(last, axis, up)  54.6 us
    psum x1, blocking collectives, body(): lax.psum((sums[0], sums[1], sums[2], sums[3], sums[4]), ('gy', 'gz'))  40.9 us
    div x30, other arithmetic, spd_solve(): answer = answer.at[row].set(value / lower[row, row])  20.1 us
    div x28, other arithmetic, spd_solve(): middle = middle.at[row].set(value / lower[row, row])  20.1 us
    ppermute x45, waiting for transfers between devices, with_halo(): after = lax.ppermute(first, axis, down)  17.2 us
    psum x1, blocking collectives, body(): lax.psum(lax.psum((sums[0], sums[1], sums[2], sums[3], sums[4]), ('gy', '...  14.1 us
  transfers between devices with their start and end apart: 90, of which 71 were waited for; matrix products, arithmetic and copies ran while one was open for 4% of the time, Pallas kernels for 0%

profile of v1, /device:TPU:0, one launch (start us, length us, event | category | flops | bytes accessed | tf_op | source)
XLA Modules:
  0.0 502.6 jit_solution(5218640193422192468)
XLA Ops:
  21.4 4.9 collective-permute-start.2
  30.6 6.1 %collective-permute-start.4 = (f32[16,4,1,130]{3,0,2,1:T(8,128)S(1)}, f32[16,4,1,130]{3,0,2,1:T(8,128)S(1)}, u32[]{:S(2)}, u32[]{:S(2)}) collective-permute-start(f32[16,4,1,130]{3,0,2,1:T(8,128)S(1)} %get-tuple-element.1207), channel_id=1, source_target_pairs={{0,1},{1,2},{2,3},{4,5},{5,6},{6,7},{8,9},{9,10},{10,11},{12,13},{... | collective-permute-start | bytes 99848 | tf_op jit(solution)/shard_map/ppermute | solution.py:14
  46.4 4.6 collective-permute-start.8
  55.6 4.8 collective-permute-start.10
  69.3 4.6 collective-permute-start.14
  78.5 4.9 collective-permute-start.16
  92.6 4.6 collective-permute-start.20
  101.1 5.0 collective-permute-start.22
  115.2 4.6 collective-permute-start.26
  123.7 5.0 collective-permute-start.28
  132.2 4.9 collective-permute-start.30
  147.9 4.6 collective-permute-start.34
  156.0 5.3 %collective-permute-start.36 = (f32[16,1,4,128]{3,0,2,1:T(8,128)S(1)}, f32[16,1,4,128]{3,0,2,1:T(8,128)S(1)}, u32[]{:S(2)}, u32[]{:S(2)}) collective-permute-start(f32[16,1,4,128]{3,0,2,1:T(8,128)S(1)} %get-tuple-element.1255), channel_id=1, source_target_pairs={{0,8},{8,16},{16,24},{1,9},{9,17},{17,25},{2,10},{10,18},{18,26},{... | collective-permute-start | bytes 98312 | tf_op jit(solution)/shard_map/ppermute | solution.py:14
  172.1 4.6 collective-permute-start.40
  180.3 5.3 %collective-permute-start.42 = (f32[16,1,4,128]{3,0,2,1:T(8,128)S(1)}, f32[16,1,4,128]{3,0,2,1:T(8,128)S(1)}, u32[]{:S(2)}, u32[]{:S(2)}) collective-permute-start(f32[16,1,4,128]{3,0,2,1:T(8,128)S(1)} %get-tuple-element.1253), channel_id=1, source_target_pairs={{0,8},{8,16},{16,24},{1,9},{9,17},{17,25},{2,10},{10,18},{18,26},{... | collective-permute-start | bytes 98312 | tf_op jit(solution)/shard_map/ppermute | solution.py:14
  196.3 4.8 collective-permute-start.46
  204.5 5.3 %collective-permute-start.48 = (f32[16,1,4,128]{3,0,2,1:T(8,128)S(1)}, f32[16,1,4,128]{3,0,2,1:T(8,128)S(1)}, u32[]{:S(2)}, u32[]{:S(2)}) collective-permute-start(f32[16,1,4,128]{3,0,2,1:T(8,128)S(1)} %get-tuple-element.1251), channel_id=1, source_target_pairs={{0,8},{8,16},{16,24},{1,9},{9,17},{17,25},{2,10},{10,18},{18,26},{... | collective-permute-start | bytes 98312 | tf_op jit(solution)/shard_map/ppermute | solution.py:14
  220.5 4.6 collective-permute-start.52
  228.7 5.3 %collective-permute-start.54 = (f32[16,1,4,128]{3,0,2,1:T(8,128)S(1)}, f32[16,1,4,128]{3,0,2,1:T(8,128)S(1)}, u32[]{:S(2)}, u32[]{:S(2)}) collective-permute-start(f32[16,1,4,128]{3,0,2,1:T(8,128)S(1)} %get-tuple-element.1249), channel_id=1, source_target_pairs={{0,8},{8,16},{16,24},{1,9},{9,17},{17,25},{2,10},{10,18},{18,26},{... | collective-permute-start | bytes 98312 | tf_op jit(solution)/shard_map/ppermute | solution.py:14
  244.8 4.6 collective-permute-start.58
  253.0 5.3 %collective-permute-start.60 = (f32[16,1,4,128]{3,0,2,1:T(8,128)S(1)}, f32[16,1,4,128]{3,0,2,1:T(8,128)S(1)}, u32[]{:S(2)}, u32[]{:S(2)}) collective-permute-start(f32[16,1,4,128]{3,0,2,1:T(8,128)S(1)} %get-tuple-element.1247), channel_id=1, source_target_pairs={{0,8},{8,16},{16,24},{1,9},{9,17},{17,25},{2,10},{10,18},{18,26},{... | collective-permute-start | bytes 98312 | tf_op jit(solution)/shard_map/ppermute | solution.py:14
  269.0 4.6 collective-permute-start.64
  277.2 5.3 %collective-permute-start.66 = (f32[16,1,4,128]{3,0,2,1:T(8,128)S(1)}, f32[16,1,4,128]{3,0,2,1:T(8,128)S(1)}, u32[]{:S(2)}, u32[]{:S(2)}) collective-permute-start(f32[16,1,4,128]{3,0,2,1:T(8,128)S(1)} %get-tuple-element.1245), channel_id=1, source_target_pairs={{0,8},{8,16},{16,24},{1,9},{9,17},{17,25},{2,10},{10,18},{18,26},{... | collective-permute-start | bytes 98312 | tf_op jit(solution)/shard_map/ppermute | solution.py:14
  293.2 4.6 collective-permute-start.70
  301.4 5.3 %collective-permute-start.72 = (f32[16,1,4,128]{3,0,2,1:T(8,128)S(1)}, f32[16,1,4,128]{3,0,2,1:T(8,128)S(1)}, u32[]{:S(2)}, u32[]{:S(2)}) collective-permute-start(f32[16,1,4,128]{3,0,2,1:T(8,128)S(1)} %get-tuple-element.1243), channel_id=1, source_target_pairs={{0,8},{8,16},{16,24},{1,9},{9,17},{17,25},{2,10},{10,18},{18,26},{... | collective-permute-start | bytes 98312 | tf_op jit(solution)/shard_map/ppermute | solution.py:14
  317.5 4.6 collective-permute-start.76
  325.6 5.3 %collective-permute-start.78 = (f32[16,1,4,128]{3,0,2,1:T(8,128)S(1)}, f32[16,1,4,128]{3,0,2,1:T(8,128)S(1)}, u32[]{:S(2)}, u32[]{:S(2)}) collective-permute-start(f32[16,1,4,128]{3,0,2,1:T(8,128)S(1)} %get-tuple-element.1241), channel_id=1, source_target_pairs={{0,8},{8,16},{16,24},{1,9},{9,17},{17,25},{2,10},{10,18},{18,26},{... | collective-permute-start | bytes 98312 | tf_op jit(solution)/shard_map/ppermute | solution.py:14
  341.7 4.6 collective-permute-start.82
  349.9 5.3 %collective-permute-start.84 = (f32[16,1,4,128]{3,0,2,1:T(8,128)S(1)}, f32[16,1,4,128]{3,0,2,1:T(8,128)S(1)}, u32[]{:S(2)}, u32[]{:S(2)}) collective-permute-start(f32[16,1,4,128]{3,0,2,1:T(8,128)S(1)} %get-tuple-element.1239), channel_id=1, source_target_pairs={{0,8},{8,16},{16,24},{1,9},{9,17},{17,25},{2,10},{10,18},{18,26},{... | collective-permute-start | bytes 98312 | tf_op jit(solution)/shard_map/ppermute | solution.py:14
  367.0 4.6 collective-permute-start.88
  374.2 40.9 %all-reduce.6 = (f32[16,16]{1,0:T(8,128)S(1)}, f32[16,16]{1,0:T(8,128)S(1)}, f32[16,16]{1,0:T(8,128)S(1)}, f32[16,16]{0,1:T(8,128)S(1)}, f32[16,16]{1,0:T(8,128)S(1)}) all-reduce(f32[16,16]{1,0:T(8,128)S(1)} %convolution_bitcast_fusion.4, ...), channel_id=1, replica_groups=mesh['gx'=4,'gy'=2,'gz'=4] {'gy','gz'}, use_global_device_ids=true, to_apply=%region_0.1 | all-reduce | flops 1280 | bytes 10240 | tf_op jit(solution)/shard_map/psum | solution.py:85
  415.0 14.1 %all-reduce.7 = (f32[16,16]{1,0:T(8,128)S(1)}, f32[16,16]{1,0:T(8,128)S(1)}, f32[16,16]{1,0:T(8,128)S(1)}, f32[16,16]{0,1:T(8,128)S(1)}, f32[16,16]{1,0:T(8,128)S(1)}) all-reduce(f32[16,16]{1,0:T(8,128)S(1)} %get-tuple-element.1161, f32[16,16]{1,0:T(8,128)S(1)} %get-tuple-element.1162, ...), channel_id=1, replica_groups=mesh['gx'=4,'gy'=2,'gz'=4] {'gx'}, use_global_device_ids=true, to_apply=%region_1.2 | all-reduce | flops 1280 | bytes 10240 | tf_op jit(solution)/shard_map/psum | solution.py:84
  (742 shorter events, 288.5 us)
Async XLA Ops:
  1.7 18.3 %collective-permute-start.1 = (f32[16,1,4,128]{3,0,2,1:T(8,128)S(1)}, f32[16,1,4,128]{3,0,2,1:T(8,128)S(1)}, u32[]{:S(2)}, u32[]{:S(2)}) collective-permute-start(f32[16,1,4,128]{3,0,2,1:T(8,128)S(1)} %get-tuple-element.1268), channel_id=1, source_target_pairs={{8,0},{16,8},{24,16},{9,1},{17,9},{25,17},{10,2},{18,10},{26,18},{... | collective-permute-start | bytes 98312 | tf_op jit(solution)/shard_map/ppermute | solution.py:15
  3.0 17.0 %collective-permute-start = (f32[16,1,4,128]{3,0,2,1:T(8,128)S(1)}, f32[16,1,4,128]{3,0,2,1:T(8,128)S(1)}, u32[]{:S(2)}, u32[]{:S(2)}) collective-permute-start(f32[16,1,4,128]{3,0,2,1:T(8,128)S(1)} %get-tuple-element.1267), channel_id=1, source_target_pairs={{0,8},{8,16},{16,24},{1,9},{9,17},{17,25},{2,10},{10,18},{18,26},{... | collective-permute-start | bytes 98312 | tf_op jit(solution)/shard_map/ppermute | solution.py:14
  20.1 7.4 %collective-permute-start.3 = (f32[16,4,4,1]{3,0,2,1:T(8,128)S(1)}, f32[16,4,4,1]{3,0,2,1:T(8,128)S(1)}, u32[]{:S(2)}, u32[]{:S(2)}) collective-permute-start(f32[16,4,4,1]{3,0,2,1:T(8,128)S(1)} %get-tuple-element.1238), channel_id=1, source_target_pairs={{4,0},{5,1},{6,2},{7,3},{12,8},{13,9},{14,10},{15,11},{20,16},{21,... | collective-permute-start | bytes 3080 | tf_op jit(solution)/shard_map/ppermute | solution.py:15
  21.4 7.8 %collective-permute-start.2 = (f32[16,4,4,1]{3,0,2,1:T(8,128)S(1)}, f32[16,4,4,1]{3,0,2,1:T(8,128)S(1)}, u32[]{:S(2)}, u32[]{:S(2)}) collective-permute-start(f32[16,4,4,1]{3,0,2,1:T(8,128)S(1)} %get-tuple-element.1237), channel_id=1, source_target_pairs={{0,4},{1,5},{2,6},{3,7},{8,12},{9,13},{10,14},{11,15},{16,20},{17,... | collective-permute-start | bytes 3080 | tf_op jit(solution)/shard_map/ppermute | solution.py:14
  29.3 7.8 %collective-permute-start.5 = (f32[16,4,1,130]{3,0,2,1:T(8,128)S(1)}, f32[16,4,1,130]{3,0,2,1:T(8,128)S(1)}, u32[]{:S(2)}, u32[]{:S(2)}) collective-permute-start(f32[16,4,1,130]{3,0,2,1:T(8,128)S(1)} %get-tuple-element.1208), channel_id=1, source_target_pairs={{1,0},{2,1},{3,2},{5,4},{6,5},{7,6},{9,8},{10,9},{11,10},{13,12},{... | collective-permute-start | bytes 99848 | tf_op jit(solution)/shard_map/ppermute | solution.py:15
  30.6 8.0 %collective-permute-start.4 = (f32[16,4,1,130]{3,0,2,1:T(8,128)S(1)}, f32[16,4,1,130]{3,0,2,1:T(8,128)S(1)}, u32[]{:S(2)}, u32[]{:S(2)}) collective-permute-start(f32[16,4,1,130]{3,0,2,1:T(8,128)S(1)} %get-tuple-element.1207), channel_id=1, source_target_pairs={{0,1},{1,2},{2,3},{4,5},{5,6},{6,7},{8,9},{9,10},{10,11},{12,13},{... | collective-permute-start | bytes 99848 | tf_op jit(solution)/shard_map/ppermute | solution.py:14
  45.1 7.9 %collective-permute-start.9 = (f32[16,4,4,1]{3,0,2,1:T(8,128)S(1)}, f32[16,4,4,1]{3,0,2,1:T(8,128)S(1)}, u32[]{:S(2)}, u32[]{:S(2)}) collective-permute-start(f32[16,4,4,1]{3,0,2,1:T(8,128)S(1)} %get-tuple-element.1236), channel_id=1, source_target_pairs={{4,0},{5,1},{6,2},{7,3},{12,8},{13,9},{14,10},{15,11},{20,16},{21,... | collective-permute-start | bytes 3080 | tf_op jit(solution)/shard_map/ppermute | solution.py:15
  46.4 7.8 %collective-permute-start.8 = (f32[16,4,4,1]{3,0,2,1:T(8,128)S(1)}, f32[16,4,4,1]{3,0,2,1:T(8,128)S(1)}, u32[]{:S(2)}, u32[]{:S(2)}) collective-permute-start(f32[16,4,4,1]{3,0,2,1:T(8,128)S(1)} %get-tuple-element.1235), channel_id=1, source_target_pairs={{0,4},{1,5},{2,6},{3,7},{8,12},{9,13},{10,14},{11,15},{16,20},{17,... | collective-permute-start | bytes 3080 | tf_op jit(solution)/shard_map/ppermute | solution.py:14
  68.0 7.4 %collective-permute-start.15 = (f32[16,4,4,1]{3,0,2,1:T(8,128)S(1)}, f32[16,4,4,1]{3,0,2,1:T(8,128)S(1)}, u32[]{:S(2)}, u32[]{:S(2)}) collective-permute-start(f32[16,4,4,1]{3,0,2,1:T(8,128)S(1)} %get-tuple-element.1234), channel_id=1, source_target_pairs={{4,0},{5,1},{6,2},{7,3},{12,8},{13,9},{14,10},{15,11},{20,16},{21,... | collective-permute-start | bytes 3080 | tf_op jit(solution)/shard_map/ppermute | solution.py:15
  69.3 7.8 %collective-permute-start.14 = (f32[16,4,4,1]{3,0,2,1:T(8,128)S(1)}, f32[16,4,4,1]{3,0,2,1:T(8,128)S(1)}, u32[]{:S(2)}, u32[]{:S(2)}) collective-permute-start(f32[16,4,4,1]{3,0,2,1:T(8,128)S(1)} %get-tuple-element.1233), channel_id=1, source_target_pairs={{0,4},{1,5},{2,6},{3,7},{8,12},{9,13},{10,14},{11,15},{16,20},{17,... | collective-permute-start | bytes 3080 | tf_op jit(solution)/shard_map/ppermute | solution.py:14
  77.2 7.2 %collective-permute-start.17 = (f32[16,4,1,130]{3,0,2,1:T(8,128)S(1)}, f32[16,4,1,130]{3,0,2,1:T(8,128)S(1)}, u32[]{:S(2)}, u32[]{:S(2)}) collective-permute-start(f32[16,4,1,130]{3,0,2,1:T(8,128)S(1)} %get-tuple-element.1204), channel_id=1, source_target_pairs={{1,0},{2,1},{3,2},{5,4},{6,5},{7,6},{9,8},{10,9},{11,10},{13,12},{... | collective-permute-start | bytes 99848 | tf_op jit(solution)/shard_map/ppermute | solution.py:15
  78.5 7.1 %collective-permute-start.16 = (f32[16,4,1,130]{3,0,2,1:T(8,128)S(1)}, f32[16,4,1,130]{3,0,2,1:T(8,128)S(1)}, u32[]{:S(2)}, u32[]{:S(2)}) collective-permute-start(f32[16,4,1,130]{3,0,2,1:T(8,128)S(1)} %get-tuple-element.1203), channel_id=1, source_target_pairs={{0,1},{1,2},{2,3},{4,5},{5,6},{6,7},{8,9},{9,10},{10,11},{12,13},{... | collective-permute-start | bytes 99848 | tf_op jit(solution)/shard_map/ppermute | solution.py:14
  91.3 6.9 %collective-permute-start.21 = (f32[16,4,4,1]{3,0,2,1:T(8,128)S(1)}, f32[16,4,4,1]{3,0,2,1:T(8,128)S(1)}, u32[]{:S(2)}, u32[]{:S(2)}) collective-permute-start(f32[16,4,4,1]{3,0,2,1:T(8,128)S(1)} %get-tuple-element.1232), channel_id=1, source_target_pairs={{4,0},{5,1},{6,2},{7,3},{12,8},{13,9},{14,10},{15,11},{20,16},{21,... | collective-permute-start | bytes 3080 | tf_op jit(solution)/shard_map/ppermute | solution.py:15
  92.6 7.1 %collective-permute-start.20 = (f32[16,4,4,1]{3,0,2,1:T(8,128)S(1)}, f32[16,4,4,1]{3,0,2,1:T(8,128)S(1)}, u32[]{:S(2)}, u32[]{:S(2)}) collective-permute-start(f32[16,4,4,1]{3,0,2,1:T(8,128)S(1)} %get-tuple-element.1231), channel_id=1, source_target_pairs={{0,4},{1,5},{2,6},{3,7},{8,12},{9,13},{10,14},{11,15},{16,20},{17,... | collective-permute-start | bytes 3080 | tf_op jit(solution)/shard_map/ppermute | solution.py:14
  101.1 7.0 %collective-permute-start.22 = (f32[16,4,1,130]{3,0,2,1:T(8,128)S(1)}, f32[16,4,1,130]{3,0,2,1:T(8,128)S(1)}, u32[]{:S(2)}, u32[]{:S(2)}) collective-permute-start(f32[16,4,1,130]{3,0,2,1:T(8,128)S(1)} %get-tuple-element.1201), channel_id=1, source_target_pairs={{0,1},{1,2},{2,3},{4,5},{5,6},{6,7},{8,9},{9,10},{10,11},{12,13},{... | collective-permute-start | bytes 99848 | tf_op jit(solution)/shard_map/ppermute | solution.py:14
  113.9 6.9 %collective-permute-start.27 = (f32[16,4,4,1]{3,0,2,1:T(8,128)S(1)}, f32[16,4,4,1]{3,0,2,1:T(8,128)S(1)}, u32[]{:S(2)}, u32[]{:S(2)}) collective-permute-start(f32[16,4,4,1]{3,0,2,1:T(8,128)S(1)} %get-tuple-element.1230), channel_id=1, source_target_pairs={{4,0},{5,1},{6,2},{7,3},{12,8},{13,9},{14,10},{15,11},{20,16},{21,... | collective-permute-start | bytes 3080 | tf_op jit(solution)/shard_map/ppermute | solution.py:15
  115.2 7.1 %collective-permute-start.26 = (f32[16,4,4,1]{3,0,2,1:T(8,128)S(1)}, f32[16,4,4,1]{3,0,2,1:T(8,128)S(1)}, u32[]{:S(2)}, u32[]{:S(2)}) collective-permute-start(f32[16,4,4,1]{3,0,2,1:T(8,128)S(1)} %get-tuple-element.1229), channel_id=1, source_target_pairs={{0,4},{1,5},{2,6},{3,7},{8,12},{9,13},{10,14},{11,15},{16,20},{17,... | collective-permute-start | bytes 3080 | tf_op jit(solution)/shard_map/ppermute | solution.py:14
  123.7 6.9 %collective-permute-start.28 = (f32[16,4,1,130]{3,0,2,1:T(8,128)S(1)}, f32[16,4,1,130]{3,0,2,1:T(8,128)S(1)}, u32[]{:S(2)}, u32[]{:S(2)}) collective-permute-start(f32[16,4,1,130]{3,0,2,1:T(8,128)S(1)} %get-tuple-element.1199), channel_id=1, source_target_pairs={{0,1},{1,2},{2,3},{4,5},{5,6},{6,7},{8,9},{9,10},{10,11},{12,13},{... | collective-permute-start | bytes 99848 | tf_op jit(solution)/shard_map/ppermute | solution.py:14
  138.1 6.9 %collective-permute-start.33 = (f32[16,4,4,1]{3,0,2,1:T(8,128)S(1)}, f32[16,4,4,1]{3,0,2,1:T(8,128)S(1)}, u32[]{:S(2)}, u32[]{:S(2)}) collective-permute-start(f32[16,4,4,1]{3,0,2,1:T(8,128)S(1)} %get-tuple-element.1228), channel_id=1, source_target_pairs={{4,0},{5,1},{6,2},{7,3},{12,8},{13,9},{14,10},{15,11},{20,16},{21,... | collective-permute-start | bytes 3080 | tf_op jit(solution)/shard_map/ppermute | solution.py:15
  139.4 7.1 %collective-permute-start.32 = (f32[16,4,4,1]{3,0,2,1:T(8,128)S(1)}, f32[16,4,4,1]{3,0,2,1:T(8,128)S(1)}, u32[]{:S(2)}, u32[]{:S(2)}) collective-permute-start(f32[16,4,4,1]{3,0,2,1:T(8,128)S(1)} %get-tuple-element.1227), channel_id=1, source_target_pairs={{0,4},{1,5},{2,6},{3,7},{8,12},{9,13},{10,14},{11,15},{16,20},{17,... | collective-permute-start | bytes 3080 | tf_op jit(solution)/shard_map/ppermute | solution.py:14
  163.6 7.1 %collective-permute-start.38 = (f32[16,4,4,1]{3,0,2,1:T(8,128)S(1)}, f32[16,4,4,1]{3,0,2,1:T(8,128)S(1)}, u32[]{:S(2)}, u32[]{:S(2)}) collective-permute-start(f32[16,4,4,1]{3,0,2,1:T(8,128)S(1)} %get-tuple-element.1225), channel_id=1, source_target_pairs={{0,4},{1,5},{2,6},{3,7},{8,12},{9,13},{10,14},{11,15},{16,20},{17,... | collective-permute-start | bytes 3080 | tf_op jit(solution)/shard_map/ppermute | solution.py:14
  187.8 7.1 %collective-permute-start.44 = (f32[16,4,4,1]{3,0,2,1:T(8,128)S(1)}, f32[16,4,4,1]{3,0,2,1:T(8,128)S(1)}, u32[]{:S(2)}, u32[]{:S(2)}) collective-permute-start(f32[16,4,4,1]{3,0,2,1:T(8,128)S(1)} %get-tuple-element.1223), channel_id=1, source_target_pairs={{0,4},{1,5},{2,6},{3,7},{8,12},{9,13},{10,14},{11,15},{16,20},{17,... | collective-permute-start | bytes 3080 | tf_op jit(solution)/shard_map/ppermute | solution.py:14
  212.1 7.1 %collective-permute-start.50 = (f32[16,4,4,1]{3,0,2,1:T(8,128)S(1)}, f32[16,4,4,1]{3,0,2,1:T(8,128)S(1)}, u32[]{:S(2)}, u32[]{:S(2)}) collective-permute-start(f32[16,4,4,1]{3,0,2,1:T(8,128)S(1)} %get-tuple-element.1221), channel_id=1, source_target_pairs={{0,4},{1,5},{2,6},{3,7},{8,12},{9,13},{10,14},{11,15},{16,20},{17,... | collective-permute-start | bytes 3080 | tf_op jit(solution)/shard_map/ppermute | solution.py:14
  227.4 7.3 %collective-permute-start.55 = (f32[16,1,4,128]{3,0,2,1:T(8,128)S(1)}, f32[16,1,4,128]{3,0,2,1:T(8,128)S(1)}, u32[]{:S(2)}, u32[]{:S(2)}) collective-permute-start(f32[16,1,4,128]{3,0,2,1:T(8,128)S(1)} %get-tuple-element.1250), channel_id=1, source_target_pairs={{8,0},{16,8},{24,16},{9,1},{17,9},{25,17},{10,2},{18,10},{26,18},{... | collective-permute-start | bytes 98312 | tf_op jit(solution)/shard_map/ppermute | solution.py:15
  236.3 7.1 %collective-permute-start.56 = (f32[16,4,4,1]{3,0,2,1:T(8,128)S(1)}, f32[16,4,4,1]{3,0,2,1:T(8,128)S(1)}, u32[]{:S(2)}, u32[]{:S(2)}) collective-permute-start(f32[16,4,4,1]{3,0,2,1:T(8,128)S(1)} %get-tuple-element.1219), channel_id=1, source_target_pairs={{0,4},{1,5},{2,6},{3,7},{8,12},{9,13},{10,14},{11,15},{16,20},{17,... | collective-permute-start | bytes 3080 | tf_op jit(solution)/shard_map/ppermute | solution.py:14
  260.5 7.1 %collective-permute-start.62 = (f32[16,4,4,1]{3,0,2,1:T(8,128)S(1)}, f32[16,4,4,1]{3,0,2,1:T(8,128)S(1)}, u32[]{:S(2)}, u32[]{:S(2)}) collective-permute-start(f32[16,4,4,1]{3,0,2,1:T(8,128)S(1)} %get-tuple-element.1217), channel_id=1, source_target_pairs={{0,4},{1,5},{2,6},{3,7},{8,12},{9,13},{10,14},{11,15},{16,20},{17,... | collective-permute-start | bytes 3080 | tf_op jit(solution)/shard_map/ppermute | solution.py:14
  284.8 7.1 %collective-permute-start.68 = (f32[16,4,4,1]{3,0,2,1:T(8,128)S(1)}, f32[16,4,4,1]{3,0,2,1:T(8,128)S(1)}, u32[]{:S(2)}, u32[]{:S(2)}) collective-permute-start(f32[16,4,4,1]{3,0,2,1:T(8,128)S(1)} %get-tuple-element.1215), channel_id=1, source_target_pairs={{0,4},{1,5},{2,6},{3,7},{8,12},{9,13},{10,14},{11,15},{16,20},{17,... | collective-permute-start | bytes 3080 | tf_op jit(solution)/shard_map/ppermute | solution.py:14
  309.0 7.1 %collective-permute-start.74 = (f32[16,4,4,1]{3,0,2,1:T(8,128)S(1)}, f32[16,4,4,1]{3,0,2,1:T(8,128)S(1)}, u32[]{:S(2)}, u32[]{:S(2)}) collective-permute-start(f32[16,4,4,1]{3,0,2,1:T(8,128)S(1)} %get-tuple-element.1213), channel_id=1, source_target_pairs={{0,4},{1,5},{2,6},{3,7},{8,12},{9,13},{10,14},{11,15},{16,20},{17,... | collective-permute-start | bytes 3080 | tf_op jit(solution)/shard_map/ppermute | solution.py:14
  333.2 7.1 %collective-permute-start.80 = (f32[16,4,4,1]{3,0,2,1:T(8,128)S(1)}, f32[16,4,4,1]{3,0,2,1:T(8,128)S(1)}, u32[]{:S(2)}, u32[]{:S(2)}) collective-permute-start(f32[16,4,4,1]{3,0,2,1:T(8,128)S(1)} %get-tuple-element.1211), channel_id=1, source_target_pairs={{0,4},{1,5},{2,6},{3,7},{8,12},{9,13},{10,14},{11,15},{16,20},{17,... | collective-permute-start | bytes 3080 | tf_op jit(solution)/shard_map/ppermute | solution.py:14
  348.6 8.4 %collective-permute-start.85 = (f32[16,1,4,128]{3,0,2,1:T(8,128)S(1)}, f32[16,1,4,128]{3,0,2,1:T(8,128)S(1)}, u32[]{:S(2)}, u32[]{:S(2)}) collective-permute-start(f32[16,1,4,128]{3,0,2,1:T(8,128)S(1)} %get-tuple-element.1240), channel_id=1, source_target_pairs={{8,0},{16,8},{24,16},{9,1},{17,9},{25,17},{10,2},{18,10},{26,18},{... | collective-permute-start | bytes 98312 | tf_op jit(solution)/shard_map/ppermute | solution.py:15
  349.9 7.2 %collective-permute-start.84 = (f32[16,1,4,128]{3,0,2,1:T(8,128)S(1)}, f32[16,1,4,128]{3,0,2,1:T(8,128)S(1)}, u32[]{:S(2)}, u32[]{:S(2)}) collective-permute-start(f32[16,1,4,128]{3,0,2,1:T(8,128)S(1)} %get-tuple-element.1239), channel_id=1, source_target_pairs={{0,8},{8,16},{16,24},{1,9},{9,17},{17,25},{2,10},{10,18},{18,26},{... | collective-permute-start | bytes 98312 | tf_op jit(solution)/shard_map/ppermute | solution.py:14
  358.5 7.1 %collective-permute-start.86 = (f32[16,4,4,1]{3,0,2,1:T(8,128)S(1)}, f32[16,4,4,1]{3,0,2,1:T(8,128)S(1)}, u32[]{:S(2)}, u32[]{:S(2)}) collective-permute-start(f32[16,4,4,1]{3,0,2,1:T(8,128)S(1)} %get-tuple-element.1209), channel_id=1, source_target_pairs={{0,4},{1,5},{2,6},{3,7},{8,12},{9,13},{10,14},{11,15},{16,20},{17,... | collective-permute-start | bytes 3080 | tf_op jit(solution)/shard_map/ppermute | solution.py:14
  (63 other events, 596.6 us)
